TPU v7x, 256 devices: a whole 4x4x8 slice. The times are simulated.
256 devices in a mesh: shards: 16 (over x, y), tensor: 4 (over z_hi, core), replica: 4 (over z_lo).
Axes of the slice: x: 4, y: 4, z: 8 (z_hi: 2, z_lo: 4; z = z_hi * 4 + z_lo), core: 2. Of those that a mesh axis runs over, the one named last changes fastest.
Arguments:
- activations: bfloat16 [262144, 1024], P(('shards', 'tensor', 'replica')), may hold values from -24 to 24
- grads_out: bfloat16 [262144, 1024], P(('shards', 'tensor', 'replica')), may hold values from -24 to 24
- grad_parts: float32 [64, 1024, 1024], P(('shards', 'replica'), None, 'tensor'), may hold values from -80 to 80
- old_factors: float32 [16, 128, 128], replicated, may hold values from -16 to 16, as said below
- block_owner: int32 [16], replicated, may hold values from 0 to 15, as said below
- weights: float32 [1024, 1024], P(('shards', 'replica'), 'tensor'), may hold values from -0.1875 to 0.1875
- momentum: float32 [1024, 1024], P(('shards', 'replica'), 'tensor'), may hold values from -4 to 4
Outputs:
- weights_next: float32 [1024, 1024], P(None, 'tensor')
- momentum_next: float32 [1024, 1024], P(('shards', 'replica'), 'tensor')
- next_factor_blocks: float32 [32, 128, 128], P('shards')
Inputs may be any that keep to these rules, and one draw needn't show every extreme that they name: `block_owner`: each shard index owns at most 2 of the 16 blocks, and some index owns exactly 2. `old_factors`: each block is symmetric and positive definite.
All inputs are finite; a program needn't handle non-finite values. Where the computation divides by a largest or mean magnitude, that divisor is 1e-20 or more.
Results may differ from a plain program's by a relative error of at most 0.0003.
Values sent between devices are 32-bit elements; how exact they have to be, the bound alone decides.
No kernel may reach another device: no remote copies, remote signals or barrier semaphores. Data moves between devices by JAX's collectives and lax.ppermute only.
A program may use at most 64 MiB of HBM per device.

v0:
```python
import jax
import jax.numpy as jnp
from jax import lax
from jax.sharding import PartitionSpec as P

NS_STEPS = 4
exact_mode = lax.Precision.HIGHEST
decay_rate = 0.75
damping = 0.1
damp_shift = 0.001
clip_norm = 256.0
momentum_rate = 0.9
step_rate = 0.05


def sample_stats(samples, block_size):
    sample_rows, width = samples.shape
    blocks = samples.reshape(sample_rows, width // block_size, block_size)
    return jnp.einsum("tnb,tnc->nbc", blocks, blocks, preferred_element_type=jnp.float32)


def build_slots(block_owner, capacity, slot_count):
    block_count = block_owner.shape[0]
    positions = jnp.arange(block_count, dtype=jnp.int32)
    earlier = (block_owner[:, None] == block_owner[None, :]) & (
        positions[None, :] < positions[:, None]
    )
    owner_slot_list = block_owner * capacity + jnp.sum(earlier.astype(jnp.int32), axis=1)
    return (owner_slot_list[None, :] == jnp.arange(slot_count, dtype=jnp.int32)[:, None]).astype(
        jnp.float32
    )


def newton_inverse(mixed_factor_blocks):
    block_size = mixed_factor_blocks.shape[-1]
    identity = jnp.eye(block_size, dtype=jnp.float32)
    traces = jnp.trace(mixed_factor_blocks, axis1=1, axis2=2)
    damped = (
        mixed_factor_blocks + (damping * traces / block_size + damp_shift)[:, None, None] * identity
    )
    bounds = jnp.max(jnp.sum(jnp.abs(damped), axis=2), axis=1)
    approx = identity[None, :, :] / bounds[:, None, None]
    for iteration in range(NS_STEPS):
        left_part = jnp.einsum("nab,nbc->nac", approx, damped, precision=exact_mode)
        approx = 2.0 * approx - jnp.einsum("nab,nbc->nac", left_part, approx, precision=exact_mode)
    return approx


def apply_right(left_part, right_inv, block_size):
    row_count, col_count = left_part.shape
    right_count = col_count // block_size
    return jnp.einsum(
        "rnb,nbc->rnc",
        left_part.reshape(row_count, right_count, block_size),
        right_inv,
        precision=exact_mode,
    ).reshape(row_count, col_count)


def body(activations, grads_out, grad_parts, old_factors, block_owner, weights, momentum):
    shard_count = lax.axis_size("shards")
    block_count = old_factors.shape[0]
    block_size = old_factors.shape[1]
    capacity = (block_count + shard_count - 1) // shard_count + 1
    slot_count = capacity * shard_count
    slot_table = build_slots(block_owner, capacity, slot_count)
    local_stats = jnp.concatenate(
        [sample_stats(activations, block_size), sample_stats(grads_out, block_size)], axis=0
    )
    packed = jnp.dot(
        slot_table, local_stats.reshape(block_count, block_size * block_size), precision=exact_mode
    )
    first_slot = lax.axis_index("shards") * capacity
    summed = lax.psum(packed, ("shards", "tensor", "replica"))
    owned = lax.dynamic_slice_in_dim(summed, first_slot, capacity, 0)
    sample_count = (
        activations.shape[0] * shard_count * lax.axis_size("tensor") * lax.axis_size("replica")
    )
    owned_table = lax.dynamic_slice_in_dim(slot_table, first_slot, capacity, 0)
    old_owned = jnp.dot(
        owned_table, old_factors.reshape(block_count, block_size * block_size), precision=exact_mode
    )
    mixed_factor_blocks = (
        decay_rate * old_owned + (1.0 - decay_rate) * (owned / sample_count)
    ).reshape(capacity, block_size, block_size)
    inverse_owned = newton_inverse(mixed_factor_blocks)
    start_blocks = jnp.zeros((block_count, block_size * block_size), jnp.float32)
    shard_piece = lax.all_gather(inverse_owned, "shards", axis=0, tiled=True)
    piece_rows = shard_piece.shape[0]
    rows_table = lax.slice_in_dim(slot_table, 0, piece_rows, axis=0)
    flat_piece = shard_piece.reshape(piece_rows, block_size * block_size)
    inverse_flat = start_blocks + jnp.einsum(
        "sb,sk->bk", rows_table, flat_piece, precision=exact_mode
    )
    inverse_blocks = inverse_flat.reshape(block_count, block_size, block_size)
    partial_grad = grad_parts[0]
    row_count, col_count = partial_grad.shape
    left_count = row_count // block_size
    right_count = col_count // block_size
    right_first = left_count + lax.axis_index("tensor") * right_count
    right_inv = lax.dynamic_slice_in_dim(inverse_blocks, right_first, right_count, 0)
    left_part = jnp.einsum(
        "nab,nbc->nac",
        inverse_blocks[:left_count],
        partial_grad.reshape(left_count, block_size, col_count),
        precision=exact_mode,
    ).reshape(row_count, col_count)
    precond = apply_right(left_part, right_inv, block_size)
    total_precond, total_grad = (
        lax.psum_scatter(precond, ("shards", "replica"), scatter_dimension=0, tiled=True),
        lax.psum_scatter(partial_grad, ("shards", "replica"), scatter_dimension=0, tiled=True),
    )
    alignment_sum = lax.psum(jnp.sum(total_precond * total_grad), ("shards", "tensor", "replica"))
    clip_scale = jnp.minimum(1.0, clip_norm / jnp.sqrt(alignment_sum))
    momentum_next = momentum_rate * momentum + clip_scale * total_precond
    weights_next = weights - step_rate * momentum_next
    gathered = lax.all_gather(weights_next, ("shards", "replica"), axis=0, tiled=True)
    return (gathered, momentum_next, mixed_factor_blocks)


def solution(mesh):
    placed = (
        P(("shards", "tensor", "replica"), None),
        P(("shards", "tensor", "replica"), None),
        P(("shards", "replica"), None, "tensor"),
        P(),
        P(),
        P(("shards", "replica"), "tensor"),
        P(("shards", "replica"), "tensor"),
    )
    return jax.shard_map(
        body,
        mesh=mesh,
        in_specs=placed,
        out_specs=(P(None, "tensor"), P(("shards", "replica"), "tensor"), P("shards", None, None)),
        check_vma=False,
    )
```

profile of v0, /device:TPU:94, one launch (start us, length us, event | category | flops | bytes accessed | tf_op | source)
XLA Modules:
  0.0 1458.4 jit_solution(3931337511195937440)
XLA Ops:
  8.1 1.0 convert_reduce_fusion
  9.1 0.9 multiply_add_fusion.7
  10.0 1.1 fusion.4
  11.0 1.1 fusion.7
  12.3 2.8 fusion.10
  15.2 259.1 %all-reduce.2.cloned.1.call-done = f32[32,16384]{1,0:T(8,128)} async-done(((f32[32,16384]{1,0:T(8,128)}), f32[32,16384]{1,0:T(8,128)}) %all-reduce.2.cloned.1.call-update) | async-done | bytes 2097168 | tf_op jit(solution)/shard_map/psum | solution.py:74
  274.3 2.3 select_reduce_fusion
  276.9 0.3 fusion.20
  279.2 0.9 convolution_subtract_fusion
  280.2 0.5 reduce-scatter.5.cloned.1.call-update
  281.0 49.9 %all-gather.3.cloned.1.call-done = f32[32,128,128]{2,1,0:T(8,128)} async-done(((f32[2,128,128]{2,1,0:T(8,128)}), f32[32,128,128]{2,1,0:T(8,128)}) %all-gather.3.cloned.1.call-update) | async-done | bytes 2097168 | tf_op jit(solution)/shard_map/all_gather | solution.py:88
  330.9 3.6 fusion.1
  334.6 2.0 fusion.17
  336.7 2.7 reshape_reshape.3
  339.6 1.0 copy-done.1
  340.6 1.1 fusion.15
  341.7 1.3 copy.33
  343.1 310.3 %reduce-scatter.5.cloned.1.call-done = f32[16,256]{1,0:T(8,128)} async-done(((f32[1024,256]{1,0:T(8,128)}), f32[16,256]{1,0:T(8,128)}) %reduce-scatter.5.cloned.1.call-update) | async-done | bytes 16400 | tf_op jit(solution)/shard_map/reduce_scatter | solution.py:111
  653.4 370.3 %reduce-scatter.3.cloned.1.call-done = f32[16,256]{1,0:T(8,128)} async-done(((f32[1024,256]{1,0:T(8,128)}), f32[16,256]{1,0:T(8,128)}) %reduce-scatter.3.cloned.1.call-update) | async-done | bytes 16400 | tf_op jit(solution)/shard_map/reduce_scatter | solution.py:110
  1023.7 1.3 multiply_reduce_fusion
  1025.0 72.1 %psum.15 = f32[]{:T(128)} all-reduce(f32[]{:T(128)} %multiply_reduce_fusion), channel_id=1, replica_groups=mesh['shards'=16,'tensor'=4,'replica'=4] {'shards','tensor','replica'}, use_global_device_ids=true, to_apply=%region_8.9 | all-reduce | flops 1 | bytes 8 | tf_op jit(solution)/shard_map/psum | solution.py:113
  1097.9 1.3 multiply_subtract_fusion
  1099.2 349.3 %all-gather.5.cloned.1.call-done = f32[1024,256]{1,0:T(8,128)} async-done(((f32[16,256]{1,0:T(8,128)}), f32[1024,256]{1,0:T(8,128)}) %all-gather.5.cloned.1.call-update) | async-done | bytes 1048592 | tf_op jit(solution)/shard_map/all_gather | solution.py:117
  1448.5 2.3 copy.72
  (39 shorter events, 3.0 us)
Async XLA Ops:
  8.0 2.0 copy-start
  8.0 266.3 %all-reduce.2.cloned.1.call-start = ((), (), s32[]{:S(2)}) async-start(), calls=%async_computation.2 | async-start | bytes 4194304 | tf_op jit(solution)/shard_map/psum | solution.py:74
  8.1 3.0 copy-start.7
  12.2 262.0 %copy-start.4 = (f32[16,128,128]{2,1,0:T(8,128)S(1)}, f32[16,128,128]{2,1,0:T(8,128)}, u32[]{:S(2)}) copy-start(f32[16,128,128]{2,1,0:T(8,128)} %param.10) | copy-start | bytes 3145732
  15.1 315.9 %all-gather.3.cloned.1.call-start = ((), (), s32[]{:S(2)}) async-start(), calls=%async_computation.3 | async-start | bytes 2228224 | tf_op jit(solution)/shard_map/all_gather | solution.py:88
  276.8 3.9 copy-start.3
  280.2 373.2 %reduce-scatter.5.cloned.1.call-start = ((), (), s32[]{:S(2)}) async-start(), calls=%async_computation.5 | async-start | bytes 1064960 | tf_op jit(solution)/shard_map/reduce_scatter | solution.py:111
  280.8 742.9 %reduce-scatter.3.cloned.1.call-start = ((), (), s32[]{:S(2)}) async-start(), calls=%async_computation.4 | async-start | bytes 1064960 | tf_op jit(solution)/shard_map/reduce_scatter | solution.py:110
  330.9 3.7 copy-start.2
  339.4 1.2 copy-start.1
  341.7 756.2 %copy-start.5 = (f32[16,256]{1,0:T(8,128)S(1)}, f32[16,256]{1,0:T(8,128)}, u32[]{:S(2)}) copy-start(f32[16,256]{1,0:T(8,128)} %param.12) | copy-start | bytes 49156
  341.7 756.2 %copy-start.6 = (f32[16,256]{1,0:T(8,128)S(1)}, f32[16,256]{1,0:T(8,128)}, u32[]{:S(2)}) copy-start(f32[16,256]{1,0:T(8,128)} %param.13) | copy-start | bytes 49156
  343.0 1105.5 %all-gather.5.cloned.1.call-start = ((), (), s32[]{:S(2)}) async-start(), calls=%async_computation.6 | async-start | bytes 1064960 | tf_op jit(solution)/shard_map/all_gather | solution.py:117
Sparse Core Ops, SparseCore 0:
  15.2 259.0 all-reduce.1
  280.3 50.6 all-gather.2
Sparse Core Ops, SparseCore 1:
  283.1 370.2 reduce-scatter.4
  656.5 367.1 reduce-scatter.2
  1099.3 349.2 all-gather.4
where the time goes:
time: 1460 us
  waiting for transfers between devices  1340 us (92%)
  blocking collectives  72.1 us (5%)
  matrix products  17.2 us (1%)
  between operations  16.6 us (1%)
    reduce_scatter x1, waiting for transfers between devices, body(): lax.psum_scatter(precond, ('shards', 'replica'), scatter_dimension=0, til...  370 us
    all_gather x1, waiting for transfers between devices, body(): lax.all_gather(weights_next, ('shards', 'replica'), axis=0, tiled=True)  349 us
    reduce_scatter x1, waiting for transfers between devices, body(): lax.psum_scatter(partial_grad, ('shards', 'replica'), scatter_dimension=0...  310 us
    psum x1, waiting for transfers between devices, body(): summed = lax.psum(packed, ('shards', 'tensor', 'replica'))  259 us
    psum x1, blocking collectives, body(): lax.psum(jnp.sum(total_precond * total_grad), ('shards', 'tensor', 'repli...  72.1 us
    all_gather x1, waiting for transfers between devices, body(): shard_piece = lax.all_gather(inverse_owned, 'shards', axis=0, tiled=True)  49.9 us
  transfers between devices with their start and end apart: 5, of which 5 were waited for; matrix products, arithmetic and copies ran while one was open for 1% of the time, Pallas kernels for 0%

commit v1 on v0

--- a/solution.py
+++ b/solution.py
@@ -114,7 +114,15 @@
     clip_scale = jnp.minimum(1.0, clip_norm / jnp.sqrt(alignment_sum))
     momentum_next = momentum_rate * momentum + clip_scale * total_precond
     weights_next = weights - step_rate * momentum_next
-    gathered = lax.all_gather(weights_next, ("shards", "replica"), axis=0, tiled=True)
+    gathered = jnp.concatenate(
+        lax.all_to_all(
+            jnp.stack([weights_next] * lax.axis_size(("shards", "replica"))),
+            concat_axis=0,
+            split_axis=0,
+            axis_name=("shards", "replica"),
+        ),
+        axis=0,
+    )
     return (gathered, momentum_next, mixed_factor_blocks)
 
 

time: 1460 us -> 1150 us (0.79)
  waiting for transfers between devices: 1340 us -> 990 us
  blocking collectives: 72.1 us -> 108 us
    all_gather x1 -> x0, waiting for transfers between devices: 349 us -> none  [body(): lax.all_gather(weights_next, ('shards', 'replica'), axis=0, tiled=True)]
    all_to_all x0 -> x1, blocking collectives: none -> 36 us  [body(): lax.all_to_all(jnp.stack([weights_next] * lax.axis_size(('shards', 'repli...]
  transfers between devices with their start and end apart: 5 -> 4, of which waited for: 5 -> 4; matrix products, arithmetic and copies ran while one was open for 1% -> 1% of each run, Pallas kernels for 0% -> 0%
where the time goes in v1:
time: 1150 us; the launch traced here: 1140 us
  waiting for transfers between devices  990 us (86%)
  blocking collectives  108 us (9%)
  matrix products  17.2 us (1%)
  between operations  16.4 us (1%)
    reduce_scatter x1, waiting for transfers between devices, body(): lax.psum_scatter(precond, ('shards', 'replica'), scatter_dimension=0, til...  370 us
    reduce_scatter x1, waiting for transfers between devices, body(): lax.psum_scatter(partial_grad, ('shards', 'replica'), scatter_dimension=0...  310 us
    psum x1, waiting for transfers between devices, body(): summed = lax.psum(packed, ('shards', 'tensor', 'replica'))  259 us
    psum x1, blocking collectives, body(): lax.psum(jnp.sum(total_precond * total_grad), ('shards', 'tensor', 'repli...  72.1 us
    all_gather x1, waiting for transfers between devices, body(): shard_piece = lax.all_gather(inverse_owned, 'shards', axis=0, tiled=True)  49.9 us
    all_to_all x1, blocking collectives, body(): lax.all_to_all(jnp.stack([weights_next] * lax.axis_size(('shards', 'repli...  36 us
  transfers between devices with their start and end apart: 4, of which 4 were waited for; matrix products, arithmetic and copies ran while one was open for 1% of the time, Pallas kernels for 0%

profile of v1, /device:TPU:94, one launch (start us, length us, event | category | flops | bytes accessed | tf_op | source)
XLA Modules:
  0.0 1143.7 jit_solution(13893582625262396883)
XLA Ops:
  8.1 1.0 convert_reduce_fusion
  9.1 0.9 multiply_add_fusion.7
  10.0 1.1 fusion.4
  11.0 1.1 fusion.7
  12.3 2.8 fusion.10
  15.2 259.1 %all-reduce.2.cloned.1.call-done = f32[32,16384]{1,0:T(8,128)} async-done(((f32[32,16384]{1,0:T(8,128)}), f32[32,16384]{1,0:T(8,128)}) %all-reduce.2.cloned.1.call-update) | async-done | bytes 2097168 | tf_op jit(solution)/shard_map/psum | solution.py:74
  274.3 2.3 select_reduce_fusion
  276.9 0.3 fusion.20
  279.2 0.9 convolution_subtract_fusion
  280.2 0.5 reduce-scatter.5.cloned.1.call-update
  281.0 49.9 %all-gather.2.cloned.1.call-done = f32[32,128,128]{2,1,0:T(8,128)} async-done(((f32[2,128,128]{2,1,0:T(8,128)}), f32[32,128,128]{2,1,0:T(8,128)}) %all-gather.2.cloned.1.call-update) | async-done | bytes 2097168 | tf_op jit(solution)/shard_map/all_gather | solution.py:88
  330.9 3.6 fusion.1
  334.6 2.0 fusion.17
  336.7 2.7 reshape_reshape.3
  339.6 1.0 copy-done.1
  340.6 1.1 fusion.15
  341.7 1.3 copy.33
  343.0 310.4 %reduce-scatter.5.cloned.1.call-done = f32[16,256]{1,0:T(8,128)} async-done(((f32[1024,256]{1,0:T(8,128)}), f32[16,256]{1,0:T(8,128)}) %reduce-scatter.5.cloned.1.call-update) | async-done | bytes 16400 | tf_op jit(solution)/shard_map/reduce_scatter | solution.py:111
  653.4 370.3 %reduce-scatter.3.cloned.1.call-done = f32[16,256]{1,0:T(8,128)} async-done(((f32[1024,256]{1,0:T(8,128)}), f32[16,256]{1,0:T(8,128)}) %reduce-scatter.3.cloned.1.call-update) | async-done | bytes 16400 | tf_op jit(solution)/shard_map/reduce_scatter | solution.py:110
  1023.7 1.3 multiply_reduce_fusion
  1025.0 72.1 %psum.15 = f32[]{:T(128)} all-reduce(f32[]{:T(128)} %multiply_reduce_fusion), channel_id=1, replica_groups=mesh['shards'=16,'tensor'=4,'replica'=4] {'shards','tensor','replica'}, use_global_device_ids=true, to_apply=%region_8.9 | all-reduce | flops 1 | bytes 8 | tf_op jit(solution)/shard_map/psum | solution.py:113
  1097.9 1.3 multiply_subtract_fusion
  1099.3 36.0 %all_to_all.5 = f32[64,16,256]{2,1,0:T(8,128)S(1)} all-to-all(f32[64,16,256]{2,1,0:T(8,128)S(1)} %stack.2), channel_id=1, replica_groups=mesh['shards'=16,'tensor'=4,'replica'=4] {'shards','replica'}, dimensions={0} | all-to-all | bytes 2097152 | tf_op jit(solution)/shard_map/all_to_all | solution.py:118
  1135.3 1.0 copy.72
  (38 shorter events, 3.1 us)
Async XLA Ops:
  8.0 2.0 copy-start
  8.0 266.3 %all-reduce.2.cloned.1.call-start = ((), (), s32[]{:S(2)}) async-start(), calls=%async_computation.3 | async-start | bytes 4194304 | tf_op jit(solution)/shard_map/psum | solution.py:74
  8.1 3.0 copy-start.7
  12.2 262.0 %copy-start.4 = (f32[16,128,128]{2,1,0:T(8,128)S(1)}, f32[16,128,128]{2,1,0:T(8,128)}, u32[]{:S(2)}) copy-start(f32[16,128,128]{2,1,0:T(8,128)} %param.10) | copy-start | bytes 3145732
  15.1 315.9 %all-gather.2.cloned.1.call-start = ((), (), s32[]{:S(2)}) async-start(), calls=%async_computation.4 | async-start | bytes 2228224 | tf_op jit(solution)/shard_map/all_gather | solution.py:88
  276.8 3.9 copy-start.3
  280.2 373.2 %reduce-scatter.5.cloned.1.call-start = ((), (), s32[]{:S(2)}) async-start(), calls=%async_computation.6 | async-start | bytes 1064960 | tf_op jit(solution)/shard_map/reduce_scatter | solution.py:111
  280.8 742.9 %reduce-scatter.3.cloned.1.call-start = ((), (), s32[]{:S(2)}) async-start(), calls=%async_computation.5 | async-start | bytes 1064960 | tf_op jit(solution)/shard_map/reduce_scatter | solution.py:110
  330.9 3.7 copy-start.2
  339.4 1.2 copy-start.1
  341.7 756.2 %copy-start.5 = (f32[16,256]{1,0:T(8,128)S(1)}, f32[16,256]{1,0:T(8,128)}, u32[]{:S(2)}) copy-start(f32[16,256]{1,0:T(8,128)} %param.12) | copy-start | bytes 49156
  341.7 756.2 %copy-start.6 = (f32[16,256]{1,0:T(8,128)S(1)}, f32[16,256]{1,0:T(8,128)}, u32[]{:S(2)}) copy-start(f32[16,256]{1,0:T(8,128)} %param.13) | copy-start | bytes 49156
Sparse Core Ops, SparseCore 0:
  15.2 259.0 all-reduce.1
  280.3 50.6 all-gather.1
Sparse Core Ops, SparseCore 1:
  283.1 370.2 reduce-scatter.4
  656.5 367.1 reduce-scatter.2
